TPU v7x, 32 devices: a whole 2x2x4 slice. The times are simulated.
32 devices in a mesh: mode: 4 (over z), samp: 4 (over x, core), pts: 2 (over y).
Axes of the slice: x: 2, y: 2, z: 4, core: 2. Of those that a mesh axis runs over, the one named last changes fastest.
Arguments:
- coefficients: bfloat16 [768, 12288], P('samp', 'mode'), may hold values from -15 to 15
- panels: bfloat16 [12288, 16384], P(('mode', 'samp'), 'pts'), may hold values from -0.02734375 to 0.02734375
- mean_field: float32 [16384], P('pts'), may hold values from -3 to 3
- load: float32 [16384], P('pts'), may hold values from 0.5 to 2
Outputs:
- standardized: float32 [768], P('samp')
All inputs are finite; a program needn't handle non-finite values.
Results may differ from a plain program's by a relative error of at most 0.0003.
Values may be sent and summed in bfloat16 or wider, within the bound.
A program may use at most 128 MiB of HBM per device.

v0:
```python
import jax
import jax.numpy as jnp
from jax import lax
from jax.sharding import PartitionSpec as P


def body(points, coefficients, panels, mean_field, load):
    rows = lax.all_gather(coefficients, "samp", axis=0, tiled=True)
    mine = lax.all_to_all(panels, "samp", split_axis=1, concat_axis=0, tiled=True)
    partial_value = jnp.dot(rows, mine, preferred_element_type=jnp.float32)
    portion = lax.psum_scatter(partial_value, "mode", scatter_dimension=1, tiled=True)
    count = portion.shape[1]
    offset = lax.axis_index("samp") * mine.shape[1] + lax.axis_index("mode") * count
    local_mean = lax.dynamic_slice_in_dim(mean_field, offset, count, 0)
    local_load = lax.dynamic_slice_in_dim(load, offset, count, 0)
    weighted = local_load[None, :] * jnp.exp(portion + local_mean[None, :])
    even = lax.broadcasted_iota(jnp.int32, (1, count), 1) % 2 == 0
    fine = jnp.sum(weighted, axis=1)
    coarse = jnp.sum(jnp.where(even, weighted, 0.0), axis=1)
    fine, coarse = lax.psum((fine, coarse), ("mode", "samp", "pts"))
    level_diff = fine / points - coarse * (2.0 / points)
    total = level_diff.shape[0]
    center = jnp.sum(level_diff) / total
    shifted = level_diff - center
    spread = jnp.sum(shifted * shifted) / total
    out = shifted / jnp.sqrt(spread + 1e-06)
    own = coefficients.shape[0]
    return lax.dynamic_slice_in_dim(out, lax.axis_index("samp") * own, own, 0)


def solution(mesh):
    in_specs = (P("samp", "mode"), P(("mode", "samp"), "pts"), P("pts"), P("pts"))

    def run(coefficients, panels, mean_field, load):

        def inner(*args):
            return body(mean_field.shape[0], *args)

        return jax.shard_map(
            inner, mesh=mesh, in_specs=in_specs, out_specs=P("samp"), check_vma=False
        )(coefficients, panels, mean_field, load)

    return run
```

profile of v0, /device:TPU:0, one launch (start us, length us, event | category | flops | bytes accessed | tf_op | source)
XLA Modules:
  0.0 390.0 jit_solution(15918582393272994374)
XLA Ops:
  6.5 16.6 %copy.5 = bf16[768,8192]{0,1:T(8,128)(2,1)} copy(bf16[768,8192]{1,0:T(8,128)(2,1)} %param.5) | data formatting | bytes 25165824 | tf_op args[1]
  23.2 6.3 %all-to-all-start = ((bf16[768,4,2048]{0,2,1:T(8,128)(2,1)}), bf16[768,4,2048]{0,2,1:T(8,128)(2,1)}, u32[]{:S(2)}, u32[]{:S(2)}) async-start(bf16[768,4,2048]{0,2,1:T(8,128)(2,1)} %bitcast.5), calls=%async_computation | async-start | bytes 25165824 | tf_op jit(solution)/shard_map/all_to_all | solution.py:9
  29.5 0.0 all-gather.2.cloned.1.call-start
  29.6 0.7 all-gather.2.cloned.1.call-update
  30.2 0.0 reduce-scatter.2.cloned.1.call-start
  30.3 163.2 %all-to-all-done = bf16[768,4,2048]{0,2,1:T(8,128)(2,1)} async-done(((bf16[768,4,2048]{0,2,1:T(8,128)(2,1)}), bf16[768,4,2048]{0,2,1:T(8,128)(2,1)}, u32[]{:S(2)}, u32[]{:S(2)}) %all-to-all-start) | async-done | bytes 12582944 | tf_op jit(solution)/shard_map/all_to_all | solution.py:9
  193.5 15.8 %copy.6 = bf16[4,768,2048]{2,1,0:T(8,128)(2,1)} copy(bf16[4,768,2048]{1,2,0:T(8,128)(2,1)} %bitcast.1) | data formatting | bytes 25165824 | tf_op jit(solution)/shard_map/all_to_all | solution.py:9
  209.3 0.0 all-gather.2.cloned.1.call-done
  209.3 15.9 %fusion.6 = f32[768,2048]{1,0:T(8,128)} fusion(bf16[768,3072]{1,0:T(8,128)(2,1)} %all-gather.2.cloned.1.call-done, bf16[3072,2048]{1,0:T(8,128)(2,1)} %bitcast.6), kind=kOutput, calls=%fused_computation.13 | convolution fusion | flops 9663676416 | bytes 23592960 | tf_op jit(solution)/shard_map/dot_general | solution.py:10
  225.1 0.0 reduce-scatter.2.cloned.1.call-update
  225.2 0.8 dynamic_slice.10
  225.9 0.8 dynamic_slice.9
  226.7 110.6 %reduce-scatter.2.cloned.1.call-done = f32[768,512]{1,0:T(8,128)} async-done(((f32[768,2048]{1,0:T(8,128)}), f32[768,512]{1,0:T(8,128)}) %reduce-scatter.2.cloned.1.call-update) | async-done | bytes 1572880 | tf_op jit(solution)/shard_map/reduce_scatter | solution.py:11
  337.3 1.8 fusion
  339.1 40.8 %all-reduce = (f32[768]{0:T(1024)S(1)}, f32[768]{0:T(1024)S(1)}) all-reduce(f32[768]{0:T(1024)S(1)} %get-tuple-element.6, f32[768]{0:T(1024)S(1)} %get-tuple-element.5), channel_id=1, replica_groups=mesh['mode'=4,'samp'=4,'pts'=2] {'mode','samp','pts'}, use_global_device_ids=true, to_apply=%region_4.5 | all-reduce | flops 1536 | bytes 12288 | tf_op jit(solution)/shard_map/psum | solution.py:20
  379.9 0.6 fusion.5
  381.2 0.6 multiply_reduce_fusion
  382.5 0.6 dynamic_slice.11
  (2 shorter events, 0.0 us)
Async XLA Ops:
  23.2 170.3 %all-to-all-start = ((bf16[768,4,2048]{0,2,1:T(8,128)(2,1)}), bf16[768,4,2048]{0,2,1:T(8,128)(2,1)}, u32[]{:S(2)}, u32[]{:S(2)}) async-start(bf16[768,4,2048]{0,2,1:T(8,128)(2,1)} %bitcast.5), calls=%async_computation | async-start | bytes 25165824 | tf_op jit(solution)/shard_map/all_to_all | solution.py:9
  29.5 179.7 %all-gather.2.cloned.1.call-start = ((), (), s32[]{:S(2)}) async-start(), calls=%async_computation.2 | async-start | bytes 5898240 | tf_op jit(solution)/shard_map/all_gather | solution.py:8
  30.2 307.0 %reduce-scatter.2.cloned.1.call-start = ((), (), s32[]{:S(2)}) async-start(), calls=%async_computation.3 | async-start | bytes 7864320 | tf_op jit(solution)/shard_map/reduce_scatter | solution.py:11
Sparse Core Ops, SparseCore 0:
  31.9 65.9 all-gather.1
  225.3 111.9 reduce-scatter.1
where the time goes:
time: 391 us; the launch traced here: 390 us
  waiting for transfers between devices  274 us (70%)
  blocking collectives  40.8 us (10%)
  local copies, waits for them, and re-layouts  34.6 us (9%)
  matrix products  15.9 us (4%)
  between operations  14.8 us (4%)
  starting transfers between devices  6.41 us (2%)
    all_to_all x1, waiting for transfers between devices, body(): lax.all_to_all(panels, 'samp', split_axis=1, concat_axis=0, tiled=True)  163 us
    reduce_scatter x1, waiting for transfers between devices, body(): lax.psum_scatter(partial_value, 'mode', scatter_dimension=1, tiled=True)  111 us
    psum x1, blocking collectives, body(): fine, coarse = lax.psum((fine, coarse), ('mode', 'samp', 'pts'))  40.8 us
    unnamed x1, local copies, waits for them, and re-layouts  16.6 us
    dot_general x1, matrix products, body(): partial_value = jnp.dot(rows, mine, preferred_element_type=jnp.float32)  15.9 us
    all_to_all x1, local copies, waits for them, and re-layouts, body(): lax.all_to_all(panels, 'samp', split_axis=1, concat_axis=0, tiled=True)  15.8 us
  transfers between devices with their start and end apart: 3, of which 2 were waited for; matrix products, arithmetic and copies ran while one was open for 4% of the time, Pallas kernels for 0%

commit v1 on v0

--- a/solution.py
+++ b/solution.py
@@ -6,7 +6,10 @@
 
 def body(points, coefficients, panels, mean_field, load):
     rows = lax.all_gather(coefficients, "samp", axis=0, tiled=True)
-    mine = lax.all_to_all(panels, "samp", split_axis=1, concat_axis=0, tiled=True)
+    mine = jnp.concatenate(
+        lax.all_to_all(jnp.stack(jnp.split(panels, lax.axis_size("samp"), axis=1)), "samp", 0, 0),
+        axis=0,
+    )
     partial_value = jnp.dot(rows, mine, preferred_element_type=jnp.float32)
     portion = lax.psum_scatter(partial_value, "mode", scatter_dimension=1, tiled=True)
     count = portion.shape[1]

time: 391 us -> 369 us (0.944)
  local copies, waits for them, and re-layouts: 34.6 us -> 7.41 us
  other arithmetic: 3.07 us -> 8.69 us
    all_to_all x1, waiting for transfers between devices: 163 us -> 95.6 us  [body(): lax.all_to_all(jnp.stack(jnp.split(panels, lax.axis_size('samp'), axis=1)...]
    all_gather x1, waiting for transfers between devices: 0.01 us -> 67.6 us  [body(): rows = lax.all_gather(coefficients, 'samp', axis=0, tiled=True)]
    unnamed x1 -> x0, local copies, waits for them, and re-layouts: 16.6 us -> none
    all_to_all x1 -> x0, local copies, waits for them, and re-layouts: 15.8 us -> none  [body(): lax.all_to_all(panels, 'samp', split_axis=1, concat_axis=0, tiled=True)]
    another operation x0 -> x1, other arithmetic: none -> 5.61 us  [body(): jnp.stack(jnp.split(panels, lax.axis_size('samp'), axis=1))]
    another operation x0 -> x1, local copies, waits for them, and re-layouts: none -> 5.25 us  [body(): jnp.stack(jnp.split(panels, lax.axis_size('samp'), axis=1))]
  transfers between devices with their start and end apart: 3 -> 3, of which waited for: 2 -> 3; matrix products, arithmetic and copies ran while one was open for 4% -> 0% of each run, Pallas kernels for 0% -> 0%
where the time goes in v1:
time: 369 us
  waiting for transfers between devices  274 us (74%)
  blocking collectives  40.8 us (11%)
  matrix products  16 us (4%)
  between operations  14.8 us (4%)
  other arithmetic  8.69 us (2%)
  local copies, waits for them, and re-layouts  7.41 us (2%)
  starting transfers between devices  6.41 us (2%)
    reduce_scatter x1, waiting for transfers between devices, body(): lax.psum_scatter(partial_value, 'mode', scatter_dimension=1, tiled=True)  111 us
    all_to_all x1, waiting for transfers between devices, body(): lax.all_to_all(jnp.stack(jnp.split(panels, lax.axis_size('samp'), axis=1)...  95.6 us
    all_gather x1, waiting for transfers between devices, body(): rows = lax.all_gather(coefficients, 'samp', axis=0, tiled=True)  67.6 us
    psum x1, blocking collectives, body(): fine, coarse = lax.psum((fine, coarse), ('mode', 'samp', 'pts'))  40.8 us
    dot_general x1, matrix products, body(): partial_value = jnp.dot(rows, mine, preferred_element_type=jnp.float32)  16 us
  transfers between devices with their start and end apart: 3, of which 3 were waited for; matrix products, arithmetic and copies ran while one was open for 0% of the time, Pallas kernels for 0%

profile of v1, /device:TPU:0, one launch (start us, length us, event | category | flops | bytes accessed | tf_op | source)
XLA Modules:
  0.0 368.6 jit_solution(13131999878667482963)
XLA Ops:
  6.5 5.2 %slice_bitcast_fusion.3 = (bf16[1,768,2048]{2,1,0:T(8,128)(2,1)S(1)}, bf16[1,768,2048]{2,1,0:T(8,128)(2,1)S(1)}, bf16[1,768,2048]{2,1,0:T(8,128)(2,1)S(1)}, bf16[1,768,2048]{2,1,0:T(8,128)(2,1)S(1)}) fusion(bf16[768,8192]{1,0:T(8,128)(2,1)} %param.5), kind=kLoop, calls=%fused_computation.5 | loop fusion | bytes 25165824 | tf_op jit(solution)/shard_map/stack | solution.py:10
  11.8 5.6 %pad_maximum_fusion = bf16[4,768,2048]{2,1,0:T(8,128)(2,1)} fusion(bf16[1,768,2048]{2,1,0:T(8,128)(2,1)S(1)} %get-tuple-element.11, bf16[1,768,2048]{2,1,0:T(8,128)(2,1)S(1)} %get-tuple-element.12, bf16[1,768,2048]{2,1,0:T(8,128)(2,1)S(1)} %get-tuple-element.10, bf16[1,768,2048]{2,1,0:T(8,128)(2,1)S(1)} %get-tuple-element.9), kind=kLoop, calls=%fused_computation | loop fusion | flops 18874368 | bytes 25165824 | tf_op jit(solution)/shard_map/stack | solution.py:10
  17.4 6.3 %all-to-all-start = ((bf16[4,768,2048]{2,1,0:T(8,128)(2,1)}), bf16[4,768,2048]{2,1,0:T(8,128)(2,1)}, u32[]{:S(2)}, u32[]{:S(2)}) async-start(bf16[4,768,2048]{2,1,0:T(8,128)(2,1)} %pad_maximum_fusion), calls=%async_computation | async-start | bytes 25165824 | tf_op jit(solution)/shard_map/all_to_all | solution.py:10
  23.7 0.0 all-gather.2.cloned.1.call-start
  23.8 0.7 all-gather.2.cloned.1.call-update
  24.5 0.0 reduce-scatter.2.cloned.1.call-start
  24.5 67.6 %all-gather.2.cloned.1.call-done = bf16[768,3072]{1,0:T(8,128)(2,1)} async-done(((bf16[192,3072]{1,0:T(8,128)(2,1)}), bf16[768,3072]{1,0:T(8,128)(2,1)}) %all-gather.2.cloned.1.call-update) | async-done | bytes 4718608 | tf_op jit(solution)/shard_map/all_gather | solution.py:8
  92.1 95.6 %all-to-all-done = bf16[4,768,2048]{2,1,0:T(8,128)(2,1)} async-done(((bf16[4,768,2048]{2,1,0:T(8,128)(2,1)}), bf16[4,768,2048]{2,1,0:T(8,128)(2,1)}, u32[]{:S(2)}, u32[]{:S(2)}) %all-to-all-start) | async-done | bytes 12582944 | tf_op jit(solution)/shard_map/all_to_all | solution.py:10
  187.7 16.0 %convolution_bitcast_fusion = f32[768,2048]{0,1:T(8,128)} fusion(bf16[3072,2048]{1,0:T(8,128)(2,1)} %bitcast.4, bf16[768,3072]{1,0:T(8,128)(2,1)} %all-gather.2.cloned.1.call-done), kind=kOutput, calls=%fused_computation.1 | convolution fusion | flops 9663676416 | bytes 23592960 | tf_op jit(solution)/shard_map/dot_general | solution.py:13
  203.8 0.0 reduce-scatter.2.cloned.1.call-update
  203.8 0.8 dynamic_slice.10
  204.5 0.8 dynamic_slice.9
  205.3 110.6 %reduce-scatter.2.cloned.1.call-done = f32[768,512]{0,1:T(8,128)} async-done(((f32[768,2048]{0,1:T(8,128)}), f32[768,512]{0,1:T(8,128)}) %reduce-scatter.2.cloned.1.call-update) | async-done | bytes 1572880 | tf_op jit(solution)/shard_map/reduce_scatter | solution.py:14
  315.9 1.9 fusion
  317.7 40.8 %all-reduce = (f32[768]{0:T(1024)S(1)}, f32[768]{0:T(1024)S(1)}) all-reduce(f32[768]{0:T(1024)S(1)} %get-tuple-element.6, f32[768]{0:T(1024)S(1)} %get-tuple-element.5), channel_id=1, replica_groups=mesh['mode'=4,'samp'=4,'pts'=2] {'mode','samp','pts'}, use_global_device_ids=true, to_apply=%region_4.5 | all-reduce | flops 1536 | bytes 12288 | tf_op jit(solution)/shard_map/psum | solution.py:23
  358.6 0.6 fusion.5
  359.8 0.6 multiply_reduce_fusion
  361.1 0.6 dynamic_slice.11
  (2 shorter events, 0.0 us)
Async XLA Ops:
  17.4 170.3 %all-to-all-start = ((bf16[4,768,2048]{2,1,0:T(8,128)(2,1)}), bf16[4,768,2048]{2,1,0:T(8,128)(2,1)}, u32[]{:S(2)}, u32[]{:S(2)}) async-start(bf16[4,768,2048]{2,1,0:T(8,128)(2,1)} %pad_maximum_fusion), calls=%async_computation | async-start | bytes 25165824 | tf_op jit(solution)/shard_map/all_to_all | solution.py:10
  23.7 68.4 %all-gather.2.cloned.1.call-start = ((), (), s32[]{:S(2)}) async-start(), calls=%async_computation.2 | async-start | bytes 5898240 | tf_op jit(solution)/shard_map/all_gather | solution.py:8
  24.5 291.4 %reduce-scatter.2.cloned.1.call-start = ((), (), s32[]{:S(2)}) async-start(), calls=%async_computation.3 | async-start | bytes 7864320 | tf_op jit(solution)/shard_map/reduce_scatter | solution.py:14
Sparse Core Ops, SparseCore 0:
  26.1 65.9 all-gather.1
  203.9 111.9 reduce-scatter.1

commit v2 on v0

--- a/solution.py
+++ b/solution.py
@@ -17,7 +17,7 @@
     even = lax.broadcasted_iota(jnp.int32, (1, count), 1) % 2 == 0
     fine = jnp.sum(weighted, axis=1)
     coarse = jnp.sum(jnp.where(even, weighted, 0.0), axis=1)
-    fine, coarse = lax.psum((fine, coarse), ("mode", "samp", "pts"))
+    fine, coarse = lax.psum(lax.psum((fine, coarse), ("samp", "pts")), "mode")
     level_diff = fine / points - coarse * (2.0 / points)
     total = level_diff.shape[0]
     center = jnp.sum(level_diff) / total

time: 391 us -> 376 us (0.962)
  blocking collectives: 40.8 us -> 25.3 us
    psum x1 -> x2, blocking collectives: 40.8 us -> 25.3 us  [body(): fine, coarse = lax.psum(lax.psum((fine, coarse), ('samp', 'pts')), 'mode')]
  transfers between devices with their start and end apart: 3 -> 3, of which waited for: 2 -> 2; matrix products, arithmetic and copies ran while one was open for 4% -> 5% of each run, Pallas kernels for 0% -> 0%
where the time goes in v2:
time: 376 us; the launch traced here: 375 us
  waiting for transfers between devices  274 us (73%)
  local copies, waits for them, and re-layouts  34.6 us (9%)
  blocking collectives  25.3 us (7%)
  matrix products  15.9 us (4%)
  between operations  14.8 us (4%)
  starting transfers between devices  6.41 us (2%)
    all_to_all x1, waiting for transfers between devices, body(): lax.all_to_all(panels, 'samp', split_axis=1, concat_axis=0, tiled=True)  163 us
    reduce_scatter x1, waiting for transfers between devices, body(): lax.psum_scatter(partial_value, 'mode', scatter_dimension=1, tiled=True)  111 us
    psum x2, blocking collectives, body(): fine, coarse = lax.psum(lax.psum((fine, coarse), ('samp', 'pts')), 'mode')  25.3 us
    unnamed x1, local copies, waits for them, and re-layouts  16.6 us
    dot_general x1, matrix products, body(): partial_value = jnp.dot(rows, mine, preferred_element_type=jnp.float32)  15.9 us
    all_to_all x1, local copies, waits for them, and re-layouts, body(): lax.all_to_all(panels, 'samp', split_axis=1, concat_axis=0, tiled=True)  15.8 us
  transfers between devices with their start and end apart: 3, of which 2 were waited for; matrix products, arithmetic and copies ran while one was open for 5% of the time, Pallas kernels for 0%

profile of v2, /device:TPU:0, one launch (start us, length us, event | category | flops | bytes accessed | tf_op | source)
XLA Modules:
  0.0 374.5 jit_solution(1017823683429696432)
XLA Ops:
  6.5 16.6 %copy.5 = bf16[768,8192]{0,1:T(8,128)(2,1)} copy(bf16[768,8192]{1,0:T(8,128)(2,1)} %param.5) | data formatting | bytes 25165824 | tf_op args[1]
  23.2 6.3 %all-to-all-start = ((bf16[768,4,2048]{0,2,1:T(8,128)(2,1)}), bf16[768,4,2048]{0,2,1:T(8,128)(2,1)}, u32[]{:S(2)}, u32[]{:S(2)}) async-start(bf16[768,4,2048]{0,2,1:T(8,128)(2,1)} %bitcast.5), calls=%async_computation | async-start | bytes 25165824 | tf_op jit(solution)/shard_map/all_to_all | solution.py:9
  29.5 0.0 all-gather.2.cloned.1.call-start
  29.6 0.7 all-gather.2.cloned.1.call-update
  30.2 0.0 reduce-scatter.2.cloned.1.call-start
  30.3 163.2 %all-to-all-done = bf16[768,4,2048]{0,2,1:T(8,128)(2,1)} async-done(((bf16[768,4,2048]{0,2,1:T(8,128)(2,1)}), bf16[768,4,2048]{0,2,1:T(8,128)(2,1)}, u32[]{:S(2)}, u32[]{:S(2)}) %all-to-all-start) | async-done | bytes 12582944 | tf_op jit(solution)/shard_map/all_to_all | solution.py:9
  193.5 15.8 %copy.6 = bf16[4,768,2048]{2,1,0:T(8,128)(2,1)} copy(bf16[4,768,2048]{1,2,0:T(8,128)(2,1)} %bitcast.1) | data formatting | bytes 25165824 | tf_op jit(solution)/shard_map/all_to_all | solution.py:9
  209.3 0.0 all-gather.2.cloned.1.call-done
  209.3 15.9 %fusion.6 = f32[768,2048]{1,0:T(8,128)} fusion(bf16[768,3072]{1,0:T(8,128)(2,1)} %all-gather.2.cloned.1.call-done, bf16[3072,2048]{1,0:T(8,128)(2,1)} %bitcast.6), kind=kOutput, calls=%fused_computation.13 | convolution fusion | flops 9663676416 | bytes 23592960 | tf_op jit(solution)/shard_map/dot_general | solution.py:10
  225.1 0.0 reduce-scatter.2.cloned.1.call-update
  225.2 0.8 dynamic_slice.10
  225.9 0.8 dynamic_slice.9
  226.7 110.6 %reduce-scatter.2.cloned.1.call-done = f32[768,512]{1,0:T(8,128)} async-done(((f32[768,2048]{1,0:T(8,128)}), f32[768,512]{1,0:T(8,128)}) %reduce-scatter.2.cloned.1.call-update) | async-done | bytes 1572880 | tf_op jit(solution)/shard_map/reduce_scatter | solution.py:11
  337.3 1.8 fusion
  339.1 14.0 %all-reduce = (f32[768]{0:T(1024)S(1)}, f32[768]{0:T(1024)S(1)}) all-reduce(f32[768]{0:T(1024)S(1)} %get-tuple-element.6, f32[768]{0:T(1024)S(1)} %get-tuple-element.5), channel_id=1, replica_groups=mesh['mode'=4,'samp'=4,'pts'=2] {'samp','pts'}, use_global_device_ids=true, to_apply=%region_5.6 | all-reduce | flops 1536 | bytes 12288 | tf_op jit(solution)/shard_map/psum | solution.py:20
  353.1 11.3 %all-reduce.1 = (f32[768]{0:T(1024)S(1)}, f32[768]{0:T(1024)S(1)}) all-reduce(f32[768]{0:T(1024)S(1)} %get-tuple-element.7, f32[768]{0:T(1024)S(1)} %get-tuple-element.8), channel_id=1, replica_groups=mesh['mode'=4,'samp'=4,'pts'=2] {'mode'}, use_global_device_ids=true, to_apply=%region_6.7 | all-reduce | flops 1536 | bytes 12288 | tf_op jit(solution)/shard_map/psum | solution.py:20
  364.5 0.6 fusion.5
  365.7 0.6 multiply_reduce_fusion
  367.0 0.6 dynamic_slice.11
  (2 shorter events, 0.0 us)
Async XLA Ops:
  23.2 170.3 %all-to-all-start = ((bf16[768,4,2048]{0,2,1:T(8,128)(2,1)}), bf16[768,4,2048]{0,2,1:T(8,128)(2,1)}, u32[]{:S(2)}, u32[]{:S(2)}) async-start(bf16[768,4,2048]{0,2,1:T(8,128)(2,1)} %bitcast.5), calls=%async_computation | async-start | bytes 25165824 | tf_op jit(solution)/shard_map/all_to_all | solution.py:9
  29.5 179.7 %all-gather.2.cloned.1.call-start = ((), (), s32[]{:S(2)}) async-start(), calls=%async_computation.2 | async-start | bytes 5898240 | tf_op jit(solution)/shard_map/all_gather | solution.py:8
  30.2 307.0 %reduce-scatter.2.cloned.1.call-start = ((), (), s32[]{:S(2)}) async-start(), calls=%async_computation.3 | async-start | bytes 7864320 | tf_op jit(solution)/shard_map/reduce_scatter | solution.py:11
Sparse Core Ops, SparseCore 0:
  31.9 65.9 all-gather.1
  225.3 111.9 reduce-scatter.1
